TPU v7x, 256 devices: a whole 4x4x8 slice. The times are simulated.
256 devices in a mesh: fsdp: 16 (over x, z_lo, core), pair: 16 (over z_hi, y).
Axes of the slice: x: 4, y: 4, z: 8 (z_hi: 4, z_lo: 2; z = z_hi * 2 + z_lo), core: 2. Of those that a mesh axis runs over, the one named last changes fastest.
Arguments:
- tokens: bfloat16 [32768, 8192], P('pair', 'fsdp'), may hold values from -6 to 6
- cotangent: bfloat16 [32768, 1024], P('pair', 'fsdp'), may hold values from -6 to 6
- value_weight: bfloat16 [8192, 1024], P('fsdp'), may hold values from -0.0625 to 0.0625
- adapter_down: bfloat16 [48, 8192, 128], P(None, 'fsdp'), may hold values from -0.0625 to 0.0625
- adapter_up: bfloat16 [48, 128, 1024], P(None, None, 'fsdp'), may hold values from -0.5 to 0.5
- pair_ids: int32 [64], P('pair'), may hold values from 0 to 47
- ranks: int32 [48], replicated, may hold values from 16 to 128, as said below
Outputs:
- input_grad: bfloat16 [32768, 8192], P('pair', 'fsdp')
- down_grad: bfloat16 [48, 8192, 128], P('pair', 'fsdp')
- up_grad: bfloat16 [48, 128, 1024], P('pair', None, 'fsdp')
Inputs may be any that keep to these rules, and one draw needn't show every extreme that they name: `ranks`: each rank is 128, 64, 32 or 16; both ends occur in every draw.
All inputs are finite; a program needn't handle non-finite values.
Results may differ from a plain program's by a relative error of at most 0.022.
Values may be sent and summed in bfloat16 or wider, within the bound.
A program may use at most 128 MiB of HBM per device.

v0:
```python
import math
import jax
import jax.numpy as jnp
from jax import lax
from jax.sharding import PartitionSpec as P


def per_device(tokens, cotangent, value_weight, adapter_down, adapter_up, pair_ids, ranks):
    rows, partial_gradient = tokens.shape
    kvpart = cotangent.shape[1]
    block_count = pair_ids.shape[0]
    block_length = rows // block_count
    npair, _, rmax = adapter_down.shape
    norm = 1.0 / math.sqrt(rows * lax.axis_size("pair"))
    columns = jnp.arange(rmax, dtype=jnp.int32)
    mask = (columns[None, :] < ranks[:, None]).astype(jnp.float32)
    scale = 32.0 / ranks.astype(jnp.float32)
    x_blocks = tokens.reshape(block_count, block_length, partial_gradient)
    c_blocks = cotangent.reshape(block_count, block_length, kvpart)
    selected_down_adapter = adapter_down[pair_ids]
    b_sel = adapter_up[pair_ids]
    low_part = jnp.einsum(
        "btd,bdr->btr", x_blocks, selected_down_adapter, preferred_element_type=jnp.float32
    )
    back_part = jnp.einsum("btk,brk->btr", c_blocks, b_sel, preferred_element_type=jnp.float32)
    low_full, back_full = (
        lax.psum(low_part.astype(jnp.bfloat16), "fsdp").astype(jnp.float32),
        lax.psum(back_part.astype(jnp.bfloat16), "fsdp").astype(jnp.float32),
    )
    rows_mask = mask[pair_ids][:, None, :]
    low_b = (low_full * rows_mask).astype(jnp.bfloat16)
    backward_up_part = (back_full * rows_mask).astype(jnp.bfloat16)
    whole_weight = lax.all_gather(value_weight, "fsdp", axis=0, tiled=True)
    cot_rows = lax.all_to_all(cotangent, "fsdp", split_axis=0, concat_axis=1, tiled=True)
    product = jnp.einsum(
        "tk,dk->td", cot_rows, whole_weight, preferred_element_type=jnp.float32
    ).astype(jnp.bfloat16)
    frozen_output = lax.all_to_all(product, "fsdp", split_axis=1, concat_axis=0, tiled=True)
    block_offset = scale[pair_ids]
    adapter_output = jnp.einsum(
        "eiz,efz->eif", backward_up_part, selected_down_adapter, preferred_element_type=jnp.float32
    )
    input_grad = (
        frozen_output.reshape(block_count, block_length, partial_gradient).astype(jnp.float32)
        + block_offset[:, None, None] * adapter_output
    ).astype(jnp.bfloat16)
    coef = block_offset * norm
    term_a = (
        jnp.einsum("btd,btr->bdr", x_blocks, backward_up_part, preferred_element_type=jnp.float32)
        * coef[:, None, None]
    )
    term_b = (
        jnp.einsum("btr,btk->brk", low_b, c_blocks, preferred_element_type=jnp.float32)
        * coef[:, None, None]
    )
    onehot = (pair_ids[:, None] == jnp.arange(npair, dtype=jnp.int32)[None, :]).astype(jnp.float32)
    part_a = jnp.einsum("bp,bdr->pdr", onehot, term_a)
    part_b = jnp.einsum("bp,brk->prk", onehot, term_b)
    down_grad, up_grad = (
        lax.psum_scatter(
            part_a.astype(jnp.bfloat16), "pair", scatter_dimension=0, tiled=True
        ).astype(jnp.float32),
        lax.psum_scatter(
            part_b.astype(jnp.bfloat16), "pair", scatter_dimension=0, tiled=True
        ).astype(jnp.float32),
    )
    return (
        input_grad.reshape(rows, partial_gradient),
        down_grad.astype(jnp.bfloat16),
        up_grad.astype(jnp.bfloat16),
    )


def solution(mesh):
    placed = (
        P("pair", "fsdp"),
        P("pair", "fsdp"),
        P("fsdp", None),
        P(None, "fsdp", None),
        P(None, None, "fsdp"),
        P("pair"),
        P(),
    )
    return jax.shard_map(
        per_device,
        mesh=mesh,
        in_specs=placed,
        out_specs=(P("pair", "fsdp"), P("pair", "fsdp", None), P("pair", None, "fsdp")),
        check_vma=False,
    )
```

profile of v0, /device:TPU:1, one launch (start us, length us, event | category | flops | bytes accessed | tf_op | source)
XLA Modules:
  0.0 455.5 jit_solution(17975335476844694819)
XLA Ops:
  7.2 0.0 copy-start
  7.2 0.0 copy-start.2
  7.2 0.0 copy-start.4
  7.2 0.0 all-reduce.3.cloned.1.call-start
  7.2 0.8 compare_select_fusion
  8.1 3.4 gather_fusion.3
  11.5 0.0 copy-start.3
  11.5 1.7 gather_fusion.1
  13.2 2.1 fusion.1
  15.3 0.0 copy-done
  15.3 1.6 fusion.2
  16.9 0.0 all-reduce.3.cloned.1.call-update
  16.9 0.0 all-gather.2.cloned.1.call-start
  17.0 0.7 all-gather.2.cloned.1.call-update
  17.7 0.0 reduce-scatter.5.cloned.1.call-start
  17.7 0.0 copy-done.4
  17.8 0.6 gather_fusion
  18.4 0.1 fusion.9
  18.5 0.6 gather_fusion.2
  19.1 126.9 %all-reduce.3.cloned.1.call-done = (bf16[4,512,128]{1,2,0:T(8,128)(2,1)}, bf16[4,512,128]{1,2,0:T(8,128)(2,1)}) async-done(((bf16[4,512,128]{1,2,0:T(8,128)(2,1)}, bf16[4,512,128]{1,2,0:T(8,128)(2,1)}), (bf16[4,512,128]{1,2,0:T(8,128)(2,1)}, bf16[4,512,128]{1,2,0:T(8,128)(2,1)})) %all-reduce.3.cloned.1.call-update) | async-done | bytes 1048592 | tf_op jit(solution)/shard_map/psum | solution.py:28
  145.9 0.0 copy-done.2
  145.9 1.4 convolution_multiply_fusion.1
  147.4 0.0 copy-done.3
  147.4 0.5 convolution_convert_fusion.2
  147.9 1.1 copy.41
  149.0 0.0 reduce-scatter.5.cloned.1.call-update
  149.0 0.0 reduce-scatter.3.cloned.1.call-start
  149.1 1.5 fusion
  150.6 1.1 copy.35
  151.7 3.0 convolution_convert_fusion.1
  154.7 4.3 copy.36
  158.9 0.0 reduce-scatter.3.cloned.1.call-update
  159.0 0.1 copy_bitcast_fusion.1
  159.0 16.1 %all_to_all.32 = bf16[16,128,64]{1,2,0:T(8,128)(2,1)S(1)} all-to-all(bf16[16,128,64]{1,2,0:T(8,128)(2,1)S(1)} %copy_bitcast_fusion.1), channel_id=1, replica_groups=mesh['fsdp'=16,'pair'=16] {'fsdp'}, dimensions={0} | all-to-all | bytes 524288 | tf_op jit(solution)/shard_map/all_to_all | solution.py:34
  175.2 70.6 %all-gather.2.cloned.1.call-done = bf16[8192,1024]{1,0:T(8,128)(2,1)} async-done(((bf16[512,1024]{1,0:T(8,128)(2,1)}), bf16[8192,1024]{1,0:T(8,128)(2,1)}) %all-gather.2.cloned.1.call-update) | async-done | bytes 16777232 | tf_op jit(solution)/shard_map/all_gather | solution.py:33
  245.8 12.8 %convolution_convert_fusion = bf16[128,8192]{1,0:T(8,128)(2,1)} fusion(bf16[128,1024]{0,1:T(8,128)(2,1)S(1)} %bitcast.47, bf16[8192,1024]{1,0:T(8,128)(2,1)} %all-gather.2.cloned.1.call-done), kind=kOutput, calls=%fused_computation.4 | convolution fusion | flops 2148532224 | bytes 19136512 | tf_op jit(solution)/shard_map/tk,dk->td/dot_general | solution.py:35
  258.5 1.8 copy.60
  260.3 35.4 %all_to_all.33 = bf16[128,16,512]{2,0,1:T(8,128)(2,1)S(1)} all-to-all(bf16[128,16,512]{2,0,1:T(8,128)(2,1)S(1)} %bitcast.44), channel_id=1, replica_groups=mesh['fsdp'=16,'pair'=16] {'fsdp'}, dimensions={1} | all-to-all | bytes 4194304 | tf_op jit(solution)/shard_map/all_to_all | solution.py:38
  295.8 0.0 copy-start.1
  295.8 0.6 convert_element_type.74
  296.3 0.5 copy-done.1
  296.8 2.4 add_convert_fusion
  299.2 36.5 %reduce-scatter.5.cloned.1.call-done = bf16[3,128,64]{1,2,0:T(8,128)(2,1)} async-done(((bf16[48,128,64]{1,2,0:T(8,128)(2,1)}), bf16[3,128,64]{1,2,0:T(8,128)(2,1)}) %reduce-scatter.5.cloned.1.call-update) | async-done | bytes 49168 | tf_op jit(solution)/shard_map/reduce_scatter | solution.py:63
  335.7 113.2 %reduce-scatter.3.cloned.1.call-done = bf16[3,512,128]{2,1,0:T(8,128)(2,1)} async-done(((bf16[48,512,128]{2,1,0:T(8,128)(2,1)}), bf16[3,512,128]{2,1,0:T(8,128)(2,1)}) %reduce-scatter.3.cloned.1.call-update) | async-done | bytes 393232 | tf_op jit(solution)/shard_map/reduce_scatter | solution.py:60
  (3 shorter events, 0.0 us)
Async XLA Ops:
  7.2 8.1 %copy-start = (bf16[2048,512]{1,0:T(8,128)(2,1)S(1)}, bf16[2048,512]{1,0:T(8,128)(2,1)}, u32[]{:S(2)}) copy-start(bf16[2048,512]{1,0:T(8,128)(2,1)} %param.7) | copy-start | bytes 6291460
  7.2 138.8 %copy-start.2 = (bf16[2048,64]{0,1:T(8,128)(2,1)S(1)}, bf16[2048,64]{0,1:T(8,128)(2,1)}, u32[]{:S(2)}) copy-start(bf16[2048,64]{0,1:T(8,128)(2,1)} %param.8) | copy-start | bytes 786436
  7.2 10.6 %copy-start.4 = (s32[48]{0:T(128)S(1)}, s32[48]{0:T(128)}, u32[]{:S(2)}) copy-start(s32[48]{0:T(128)} %param.13) | copy-start | bytes 580
  7.2 138.7 %all-reduce.3.cloned.1.call-start = ((), (), s32[]{:S(2)}) async-start(), calls=%async_computation.7 | async-start | bytes 2097152 | tf_op jit(solution)/shard_map/psum | solution.py:28
  11.5 135.9 %copy-start.3 = (s32[4]{0:T(128)S(1)}, s32[4]{0:T(128)}, u32[]{:S(2)}) copy-start(s32[4]{0:T(128)} %param.12) | copy-start | bytes 52
  16.9 228.8 %all-gather.2.cloned.1.call-start = ((), (), s32[]{:S(2)}) async-start(), calls=%async_computation.4 | async-start | bytes 17825792 | tf_op jit(solution)/shard_map/all_gather | solution.py:33
  17.7 318.0 %reduce-scatter.5.cloned.1.call-start = ((), (), s32[]{:S(2)}) async-start(), calls=%async_computation.6 | async-start | bytes 835584 | tf_op jit(solution)/shard_map/reduce_scatter | solution.py:63
  149.0 299.9 %reduce-scatter.3.cloned.1.call-start = ((), (), s32[]{:S(2)}) async-start(), calls=%async_computation.5 | async-start | bytes 6684672 | tf_op jit(solution)/shard_map/reduce_scatter | solution.py:60
  295.8 1.0 copy-start.1
Sparse Core Ops, SparseCore 0:
  17.1 128.8 all-reduce.2
  147.8 97.9 all-gather.1
  249.8 85.8 reduce-scatter.4
  339.9 109.0 reduce-scatter.2
where the time goes:
time: 456 us; the launch traced here: 455 us
  waiting for transfers between devices  348 us (76%)
  blocking collectives  51.6 us (11%)
  matrix products  25.3 us (6%)
  local copies, waits for them, and re-layouts  15.2 us (3%)
  between operations  13.9 us (3%)
    psum x1, waiting for transfers between devices, per_device(): lax.psum(back_part.astype(jnp.bfloat16), 'fsdp').astype(jnp.float32)  127 us
    reduce_scatter x1, waiting for transfers between devices, per_device(): lax.psum_scatter(part_a.astype(jnp.bfloat16), 'pair', scatter_dimension=0...  113 us
    all_gather x1, waiting for transfers between devices, per_device(): whole_weight = lax.all_gather(value_weight, 'fsdp', axis=0, tiled=True)  70.6 us
    reduce_scatter x1, waiting for transfers between devices, per_device(): lax.psum_scatter(part_b.astype(jnp.bfloat16), 'pair', scatter_dimension=0...  36.5 us
    all_to_all x1, blocking collectives, per_device(): lax.all_to_all(product, 'fsdp', split_axis=1, concat_axis=0, tiled=True)  35.4 us
    all_to_all x1, blocking collectives, per_device(): lax.all_to_all(cotangent, 'fsdp', split_axis=0, concat_axis=1, tiled=True)  16.1 us
    dot_general x1, matrix products, per_device(): jnp.einsum('tk,dk->td', cot_rows, whole_weight, preferred_element_type=jn...  12.8 us
  transfers between devices with their start and end apart: 4, of which 4 were waited for; matrix products, arithmetic and copies ran while one was open for 7% of the time, Pallas kernels for 0%

commit v1 on v0

--- a/solution.py
+++ b/solution.py
@@ -1,8 +1,21 @@
+import functools
 import math
 import jax
 import jax.numpy as jnp
 from jax import lax
 from jax.sharding import PartitionSpec as P
+
+
+def play_the_joints(u, dim_i):
+    return jnp.concatenate(
+        lax.all_to_all(
+            jnp.stack(tuple((u for _ in range(lax.axis_size("fsdp")))), axis=0), "fsdp", 0, 0
+        ),
+        axis=dim_i,
+    )
+
+
+panel_try_all = functools.partial(play_the_joints, dim_i=0)
 
 
 def per_device(tokens, cotangent, value_weight, adapter_down, adapter_up, pair_ids, ranks):
@@ -30,7 +43,7 @@
     rows_mask = mask[pair_ids][:, None, :]
     low_b = (low_full * rows_mask).astype(jnp.bfloat16)
     backward_up_part = (back_full * rows_mask).astype(jnp.bfloat16)
-    whole_weight = lax.all_gather(value_weight, "fsdp", axis=0, tiled=True)
+    whole_weight = panel_try_all(value_weight)
     cot_rows = lax.all_to_all(cotangent, "fsdp", split_axis=0, concat_axis=1, tiled=True)
     product = jnp.einsum(
         "tk,dk->td", cot_rows, whole_weight, preferred_element_type=jnp.float32

time: 456 us -> 394 us (0.86)
  waiting for transfers between devices: 348 us -> 276 us
  local copies, waits for them, and re-layouts: 15.2 us -> 22.4 us
  starting transfers between devices: 0.16 us -> 6.05 us
    all_gather x1 -> x0, waiting for transfers between devices: 70.6 us -> none  [per_device(): whole_weight = lax.all_gather(value_weight, 'fsdp', axis=0, tiled=True)]
    all_to_all x0 -> x1, waiting for transfers between devices: none -> 54.9 us  [play_the_joints(): lax.all_to_all(jnp.stack(tuple((u for _ in range(lax.axis_size('fsdp'))))...]
    reduce_scatter x1, waiting for transfers between devices: 36.5 us -> 0.01 us  [per_device(): lax.psum_scatter(part_b.astype(jnp.bfloat16), 'pair', scatter_dimension=0...]
    reduce_scatter x1, waiting for transfers between devices: 113 us -> 85.3 us  [per_device(): lax.psum_scatter(part_a.astype(jnp.bfloat16), 'pair', scatter_dimension=0...]
    psum x1, waiting for transfers between devices: 127 us -> 136 us  [per_device(): lax.psum(back_part.astype(jnp.bfloat16), 'fsdp').astype(jnp.float32)]
    another operation x0 -> x1, local copies, waits for them, and re-layouts: none -> 6.9 us  [play_the_joints(): jnp.stack(tuple((u for _ in range(lax.axis_size('fsdp')))), axis=0)]
    all_to_all x0 -> x1, starting transfers between devices: none -> 5.92 us  [play_the_joints(): lax.all_to_all(jnp.stack(tuple((u for _ in range(lax.axis_size('fsdp'))))...]
  transfers between devices with their start and end apart: 4 -> 4, of which waited for: 4 -> 3; matrix products, arithmetic and copies ran while one was open for 7% -> 10% of each run, Pallas kernels for 0% -> 0%
where the time goes in v1:
time: 394 us; the launch traced here: 393 us
  waiting for transfers between devices  276 us (70%)
  blocking collectives  50.3 us (13%)
  matrix products  23.4 us (6%)
  local copies, waits for them, and re-layouts  22.4 us (6%)
  between operations  13.9 us (4%)
  starting transfers between devices  6.05 us (2%)
    psum x1, waiting for transfers between devices, per_device(): lax.psum(back_part.astype(jnp.bfloat16), 'fsdp').astype(jnp.float32)  136 us
    reduce_scatter x1, waiting for transfers between devices, per_device(): lax.psum_scatter(part_a.astype(jnp.bfloat16), 'pair', scatter_dimension=0...  85.3 us
    all_to_all x1, waiting for transfers between devices, play_the_joints(): lax.all_to_all(jnp.stack(tuple((u for _ in range(lax.axis_size('fsdp'))))...  54.9 us
    all_to_all x1, blocking collectives, per_device(): lax.all_to_all(product, 'fsdp', split_axis=1, concat_axis=0, tiled=True)  36.2 us
    all_to_all x1, blocking collectives, per_device(): lax.all_to_all(cotangent, 'fsdp', split_axis=0, concat_axis=1, tiled=True)  14.1 us
    dot_general x1, matrix products, per_device(): jnp.einsum('tk,dk->td', cot_rows, whole_weight, preferred_element_type=jn...  12.7 us
  transfers between devices with their start and end apart: 4, of which 3 were waited for; matrix products, arithmetic and copies ran while one was open for 10% of the time, Pallas kernels for 0%

profile of v1, /device:TPU:1, one launch (start us, length us, event | category | flops | bytes accessed | tf_op | source)
XLA Modules:
  0.0 393.0 jit_solution(2652157736776624010)
XLA Ops:
  7.2 0.0 copy-start
  7.2 1.2 copy_bitcast_fusion.1
  8.3 14.1 %all_to_all.37 = bf16[16,128,64]{1,2,0:T(8,128)(2,1)S(1)} all-to-all(bf16[16,128,64]{1,2,0:T(8,128)(2,1)S(1)} %copy_bitcast_fusion.1), channel_id=1, replica_groups=mesh['fsdp'=16,'pair'=16] {'fsdp'}, dimensions={0} | all-to-all | bytes 524288 | tf_op jit(solution)/shard_map/all_to_all | solution.py:47
  22.5 6.9 %stack.2 = bf16[16,512,1024]{2,1,0:T(8,128)(2,1)} broadcast(bf16[512,1024]{1,0:T(8,128)(2,1)} %param.9), dimensions={1,2} | broadcast | bytes 17825792 | tf_op jit(solution)/shard_map/stack | solution.py:12
  29.4 0.0 copy-start.4
  29.4 0.0 copy-start.3
  29.4 5.9 %all-to-all-start.1 = ((bf16[16,512,1024]{2,1,0:T(8,128)(2,1)}), bf16[16,512,1024]{2,1,0:T(8,128)(2,1)}, u32[]{:S(2)}, u32[]{:S(2)}) async-start(bf16[16,512,1024]{2,1,0:T(8,128)(2,1)} %stack.2), calls=%async_computation.1 | async-start | bytes 33554432 | tf_op jit(solution)/shard_map/all_to_all | solution.py:11
  35.3 0.0 copy-start.5
  35.3 0.0 all-reduce.3.cloned.1.call-start
  35.4 0.0 copy-done.4
  35.4 3.4 gather_fusion.3
  38.9 1.7 gather_fusion.1
  40.6 0.0 copy-done.3
  40.6 1.1 fusion.1
  41.7 0.0 copy-done
  41.7 1.7 fusion.2
  43.4 0.0 all-reduce.3.cloned.1.call-update
  43.4 0.0 reduce-scatter.5.cloned.1.call-start
  43.4 0.0 copy-done.5
  43.5 0.6 gather_fusion
  44.1 0.1 fusion.9
  44.2 0.6 gather_fusion.2
  44.7 136.0 %all-reduce.3.cloned.1.call-done = (bf16[4,512,128]{1,2,0:T(8,128)(2,1)}, bf16[4,512,128]{1,2,0:T(8,128)(2,1)}) async-done(((bf16[4,512,128]{1,2,0:T(8,128)(2,1)}, bf16[4,512,128]{1,2,0:T(8,128)(2,1)}), (bf16[4,512,128]{1,2,0:T(8,128)(2,1)}, bf16[4,512,128]{1,2,0:T(8,128)(2,1)})) %all-reduce.3.cloned.1.call-update) | async-done | bytes 1048592 | tf_op jit(solution)/shard_map/psum | solution.py:41
  180.7 1.4 convolution_multiply_fusion.1
  182.2 0.5 convolution_convert_fusion.2
  182.7 1.1 copy.41
  183.8 0.0 reduce-scatter.5.cloned.1.call-update
  183.9 0.0 reduce-scatter.3.cloned.1.call-start
  183.9 1.5 fusion
  185.4 0.3 copy.35
  185.8 1.9 convolution_convert_fusion.1
  187.7 4.2 %copy.36 = bf16[48,512,128]{2,1,0:T(8,128)(2,1)} copy(bf16[48,512,128]{2,0,1:T(8,128)(2,1)S(1)} %convolution_convert_fusion.1) | data formatting | bytes 12582912 | tf_op jit(solution)/shard_map/convert_element_type | solution.py:74
  191.9 0.0 reduce-scatter.3.cloned.1.call-update
  191.9 54.9 %all-to-all-done.1 = bf16[16,512,1024]{2,1,0:T(8,128)(2,1)} async-done(((bf16[16,512,1024]{2,1,0:T(8,128)(2,1)}), bf16[16,512,1024]{2,1,0:T(8,128)(2,1)}, u32[]{:S(2)}, u32[]{:S(2)}) %all-to-all-start.1) | async-done | bytes 16777248 | tf_op jit(solution)/shard_map/all_to_all | solution.py:11
  246.9 12.7 %convolution_convert_fusion = bf16[128,8192]{1,0:T(8,128)(2,1)} fusion(bf16[128,1024]{0,1:T(8,128)(2,1)S(1)} %bitcast.48, bf16[8192,1024]{1,0:T(8,128)(2,1)} %bitcast.2), kind=kOutput, calls=%fused_computation.4 | convolution fusion | flops 2148532224 | bytes 19136512 | tf_op jit(solution)/shard_map/tk,dk->td/dot_general | solution.py:48
  259.6 1.8 copy.60
  261.4 36.2 %all_to_all.38 = bf16[128,16,512]{2,0,1:T(8,128)(2,1)S(1)} all-to-all(bf16[128,16,512]{2,0,1:T(8,128)(2,1)S(1)} %bitcast.45), channel_id=1, replica_groups=mesh['fsdp'=16,'pair'=16] {'fsdp'}, dimensions={1} | all-to-all | bytes 4194304 | tf_op jit(solution)/shard_map/all_to_all | solution.py:51
  297.6 0.0 copy-start.2
  297.6 0.0 copy-start.1
  297.6 0.6 convert_element_type.74
  298.2 0.5 copy-done.2
  298.7 2.4 add_convert_fusion
  301.1 0.0 reduce-scatter.5.cloned.1.call-done
  301.1 85.3 %reduce-scatter.3.cloned.1.call-done = bf16[3,512,128]{2,1,0:T(8,128)(2,1)} async-done(((bf16[48,512,128]{2,1,0:T(8,128)(2,1)}), bf16[3,512,128]{2,1,0:T(8,128)(2,1)}) %reduce-scatter.3.cloned.1.call-update) | async-done | bytes 393232 | tf_op jit(solution)/shard_map/reduce_scatter | solution.py:73
  386.4 0.0 copy-done.1
  (4 shorter events, 0.0 us)
Async XLA Ops:
  7.2 34.5 %copy-start = (bf16[2048,512]{1,0:T(8,128)(2,1)S(1)}, bf16[2048,512]{1,0:T(8,128)(2,1)}, u32[]{:S(2)}) copy-start(bf16[2048,512]{1,0:T(8,128)(2,1)} %param.7) | copy-start | bytes 6291460
  29.4 6.0 %copy-start.4 = (s32[4]{0:T(128)S(1)}, s32[4]{0:T(128)}, u32[]{:S(2)}) copy-start(s32[4]{0:T(128)} %param.12) | copy-start | bytes 52
  29.4 11.2 %copy-start.3 = (bf16[2048,64]{0,1:T(8,128)(2,1)S(1)}, bf16[2048,64]{0,1:T(8,128)(2,1)}, u32[]{:S(2)}) copy-start(bf16[2048,64]{0,1:T(8,128)(2,1)} %param.8) | copy-start | bytes 786436
  29.4 217.5 %all-to-all-start.1 = ((bf16[16,512,1024]{2,1,0:T(8,128)(2,1)}), bf16[16,512,1024]{2,1,0:T(8,128)(2,1)}, u32[]{:S(2)}, u32[]{:S(2)}) async-start(bf16[16,512,1024]{2,1,0:T(8,128)(2,1)} %stack.2), calls=%async_computation.1 | async-start | bytes 33554432 | tf_op jit(solution)/shard_map/all_to_all | solution.py:11
  35.3 8.1 %copy-start.5 = (s32[48]{0:T(128)S(1)}, s32[48]{0:T(128)}, u32[]{:S(2)}) copy-start(s32[48]{0:T(128)} %param.13) | copy-start | bytes 580
  35.3 145.4 %all-reduce.3.cloned.1.call-start = ((), (), s32[]{:S(2)}) async-start(), calls=%async_computation.7 | async-start | bytes 2097152 | tf_op jit(solution)/shard_map/psum | solution.py:41
  43.4 257.8 %reduce-scatter.5.cloned.1.call-start = ((), (), s32[]{:S(2)}) async-start(), calls=%async_computation.6 | async-start | bytes 835584 | tf_op jit(solution)/shard_map/reduce_scatter | solution.py:76
  183.9 202.6 %reduce-scatter.3.cloned.1.call-start = ((), (), s32[]{:S(2)}) async-start(), calls=%async_computation.5 | async-start | bytes 6684672 | tf_op jit(solution)/shard_map/reduce_scatter | solution.py:73
  297.6 1.1 copy-start.2
  297.6 88.8 %copy-start.1 = (bf16[2048,512]{1,0:T(8,128)(2,1)S(1)}, bf16[2048,512]{1,0:T(8,128)(2,1)}, u32[]{:S(2)}) copy-start(bf16[2048,512]{1,0:T(8,128)(2,1)} %param.7) | copy-start | bytes 6291460
Sparse Core Ops, SparseCore 0:
  43.5 137.1 all-reduce.2
  184.8 86.6 reduce-scatter.4
  275.8 110.5 reduce-scatter.2
